TPU v7x, 512 devices: a whole 4x8x8 slice. The times are simulated.
512 devices in a mesh: seq: 128 (over x, y_hi, z, core), tp: 4 (over y_lo).
Axes of the slice: x: 4, y: 8 (y_hi: 2, y_lo: 4; y = y_hi * 4 + y_lo), z: 8, core: 2. Of those that a mesh axis runs over, the one named last changes fastest.
Arguments:
- tokens: bfloat16 [16384, 2560], P('seq', 'tp'), may hold values from -6 to 6
- seg_ids: int32 [16384], P('seq'), may hold values from 0 to 31, never falling along the last dimension, each value on 1 to 4096 neighbouring positions
- norm_gain: bfloat16 [2560], replicated, may hold values from 0.099609375 to 1.8984375
- w_query: bfloat16 [2560, 2048], P('seq', 'tp'), may hold values from -3 to 3
- w_keyval: bfloat16 [2560, 512], P('seq'), may hold values from -1 to 1
- w_out: bfloat16 [2048, 2560], P('tp', 'seq'), may hold values from -0.125 to 0.125
Outputs:
- hidden: bfloat16 [16384, 2560], P('seq', 'tp')
- kv_cache: bfloat16 [16384, 512], P('seq')
Inputs may be any that keep to these rules, and one draw needn't show every extreme that they name: `seg_ids`: ids never fall along the stream; each of the 32 requests holds 1 to 4096 consecutive tokens, one exactly 4096.
All inputs are finite; a program needn't handle non-finite values.
Results may differ from a plain program's by a relative error of at most 0.0085.
Values may be sent and summed in bfloat16 or wider, within the bound.
No kernel may reach another device: no remote copies, remote signals or barrier semaphores. Data moves between devices by JAX's collectives and lax.ppermute only.
A program may use at most 64 MiB of HBM per device.

v0:
```python
import jax
import jax.numpy as jnp
from jax import lax
from jax.sharding import PartitionSpec as P

HD = 256
WINDOW = 2048
SEG_MEAN = 512


def from_behind(x, axis, by):
    devices = lax.axis_size(axis)
    pairs = [(i, i + by) for i in range(devices) if 0 <= i + by < devices]
    return lax.ppermute(x, axis, pairs)


def rms_norm(values, gain):
    wide = values.astype(jnp.float32)
    scaled = wide * lax.rsqrt(jnp.mean(wide * wide, axis=-1, keepdims=True) + 1e-06)
    return (scaled * gain.astype(jnp.float32)).astype(jnp.bfloat16)


def rotate(tensor, positions):
    quarter = tensor.shape[-1] // 4
    freq = 10000.0 ** (-jnp.arange(quarter, dtype=jnp.float32) / quarter)
    angle = positions[:, None, None] * freq
    cosine = jnp.cos(angle)
    sine = jnp.sin(angle)
    first = tensor[..., :quarter]
    second = tensor[..., quarter : 2 * quarter]
    return jnp.concatenate(
        [
            first * cosine - second * sine,
            second * cosine + first * sine,
            tensor[..., 2 * quarter :],
        ],
        axis=-1,
    )


def per_device(tokens, seg_ids, norm_gain, w_query, w_keyval, w_out):
    tok_rows = tokens.shape[0]
    seq_count = lax.axis_size("seq")
    my_index = lax.axis_index("seq")
    gathered = lax.all_gather(tokens, "tp", axis=1, tiled=True)
    normed = rms_norm(gathered, norm_gain)
    seg_total = tok_rows * seq_count // SEG_MEAN
    labels = jnp.arange(seg_total, dtype=jnp.int32)
    below = jnp.sum((seg_ids[None, :] < labels[:, None]).astype(jnp.int32), axis=1)
    starts = lax.psum(below, "seq")
    own_start = jnp.sum(jnp.where(seg_ids[:, None] == labels[None, :], starts[None, :], 0), axis=1)
    token_index = my_index * tok_rows + jnp.arange(tok_rows, dtype=jnp.int32)
    positions = (token_index - own_start).astype(jnp.float32)
    query_raw = jnp.dot(
        normed,
        lax.all_gather(w_query, "seq", axis=0, tiled=True),
        preferred_element_type=jnp.float32,
    )
    keyval_raw = jnp.dot(
        normed,
        lax.all_gather(w_keyval, "seq", axis=0, tiled=True),
        preferred_element_type=jnp.float32,
    )
    local_heads = w_query.shape[1] // HD
    queries = rotate(query_raw.reshape(tok_rows, local_heads, HD), positions).astype(jnp.bfloat16)
    key_rows = rotate(keyval_raw[:, None, :HD], positions)[:, 0, :]
    kv_cache = jnp.concatenate([key_rows, keyval_raw[:, HD:]], axis=1).astype(jnp.bfloat16)
    reach = min(WINDOW // tok_rows, seq_count - 1)

    def advance(counter, state):
        current, current_seg, store, store_seg = state
        current, current_seg = from_behind((current, current_seg), "seq", 1)
        slot = reach - 1 - counter
        store = lax.dynamic_update_slice_in_dim(store, current[None], slot, 0)
        store_seg = lax.dynamic_update_slice_in_dim(store_seg, current_seg[None], slot, 0)
        return (current, current_seg, store, store_seg)

    store_init = jnp.zeros((reach, tok_rows, kv_cache.shape[1]), jnp.bfloat16)
    seg_init = jnp.zeros((reach, tok_rows), jnp.int32)
    final_state = lax.fori_loop(0, reach, advance, (kv_cache, seg_ids, store_init, seg_init))
    block_kv = jnp.concatenate(
        [final_state[2].reshape(reach * tok_rows, kv_cache.shape[1]), kv_cache], axis=0
    )
    block_seg = jnp.concatenate([final_state[3].reshape(reach * tok_rows), seg_ids], axis=0)
    key_index = (my_index - reach) * tok_rows + jnp.arange((reach + 1) * tok_rows, dtype=jnp.int32)
    live = (block_seg[None, :] == seg_ids[:, None]) & (key_index[None, :] <= token_index[:, None])
    live = live & (token_index[:, None] - key_index[None, :] < WINDOW) & (key_index[None, :] >= 0)
    all_keys = block_kv[:, :HD]
    all_values = block_kv[:, HD:]
    head_outputs = []
    for head_idx in range(local_heads):
        scores = lax.dot_general(
            queries[:, head_idx, :],
            all_keys,
            (((1,), (1,)), ((), ())),
            preferred_element_type=jnp.float32,
        ) * HD ** (-0.5)
        scores = jnp.where(live, scores, -1e30)
        peak = jnp.max(scores, axis=1, keepdims=True)
        powered = jnp.exp(scores - peak)
        weights = (powered / jnp.sum(powered, axis=1, keepdims=True)).astype(jnp.bfloat16)
        head_outputs.append(
            jnp.dot(weights, all_values, preferred_element_type=jnp.float32).astype(jnp.bfloat16)
        )
    attended = jnp.concatenate(head_outputs, axis=1)
    partial_value = jnp.dot(
        attended,
        lax.all_gather(w_out, "seq", axis=1, tiled=True),
        preferred_element_type=jnp.float32,
    )
    summed = lax.psum_scatter(
        partial_value.astype(jnp.bfloat16), "tp", scatter_dimension=1, tiled=True
    ).astype(jnp.float32)
    hidden = (tokens.astype(jnp.float32) + summed).astype(jnp.bfloat16)
    return (hidden, kv_cache)


def solution(mesh):
    in_specs = (P("seq", "tp"), P("seq"), P(), P("seq", "tp"), P("seq", None), P("tp", "seq"))
    out_specs = (P("seq", "tp"), P("seq", None))
    return jax.shard_map(
        per_device, mesh=mesh, in_specs=in_specs, out_specs=out_specs, check_vma=False
    )
```

profile of v0, /device:TPU:2, one launch (start us, length us, event | category | flops | bytes accessed | tf_op | source)
XLA Modules:
  0.0 562.5 jit_solution(2328956909194726290)
XLA Ops:
  10.2 18.5 %all_gather.12 = bf16[128,2560]{1,0:T(8,128)(2,1)S(1)} all-gather(bf16[128,640]{1,0:T(8,128)(2,1)} %param.8), channel_id=1, replica_groups=mesh['seq'=128,'tp'=4] {'tp'}, dimensions={1}, use_global_device_ids=true | all-gather | bytes 819200 | tf_op jit(solution)/shard_map/all_gather | solution.py:45
  28.9 31.9 %psum.7 = s32[32]{0:T(128)S(1)} all-reduce(s32[32]{0:T(128)S(1)} %convert_reduce_fusion), channel_id=1, replica_groups=mesh['seq'=128,'tp'=4] {'seq'}, use_global_device_ids=true, to_apply=%region_2.0 | all-reduce | flops 32 | bytes 256 | tf_op jit(solution)/shard_map/psum | solution.py:50
  62.4 85.6 %all-gather.7.cloned.1.call-done = bf16[128,20,512]{2,1,0:T(8,128)(2,1)} async-done(((bf16[1,20,512]{2,1,0:T(8,128)(2,1)}), bf16[128,20,512]{2,1,0:T(8,128)(2,1)}) %all-gather.7.cloned.1.call-update) | async-done | bytes 2621456 | tf_op jit(solution)/shard_map/all_gather | solution.py:61
  148.0 3.6 reshape.164
  154.9 125.2 %all-gather.9.cloned.1.call-done = bf16[128,20,512]{2,1,0:T(8,128)(2,1)} async-done(((bf16[1,20,512]{2,1,0:T(8,128)(2,1)}), bf16[128,20,512]{2,1,0:T(8,128)(2,1)}) %all-gather.9.cloned.1.call-update) | async-done | bytes 2621456 | tf_op jit(solution)/shard_map/all_gather | solution.py:56
  280.1 3.6 reshape.166
  287.7 223.8 %while.19 = (s32[]{:T(128)}, bf16[128,512]{1,0:T(8,128)(2,1)S(1)}, s32[128]{0:T(128)S(1)}, bf16[16,128,512]{2,1,0:T(8,128)(2,1)S(1)}, s32[16,128]{1,0:T(8,128)S(...) while((s32[]{:T(128)}, bf16[128,512]{1,0:T(8,128)(2,1)S(1)}, s32[128]{0:T(128)S(1)}, ...), condition=%wide.region_5.6_spmd, body=%wide.region_4.5_spmd.sunk | while | flops 6 | bytes 1052899 | solution.py:80
  287.7 2.3 collective-permute-start
  289.9 2.4 collective-permute-start.1
  292.3 9.4 %collective-permute-done.1 = s32[128]{0:T(128)S(1)} collective-permute-done((s32[128]{0:T(128)S(1)}, s32[128]{0:T(128)S(1)}, u32[]{:S(2)}, u32[]{:S(2)}) %collective-permute-start.1) | collective-permute-done | bytes 544 | tf_op jit(solution)/shard_map/while/body/eval_jaxpr/ppermute | solution.py:14
  301.8 1.9 collective-permute-start
  303.8 1.9 collective-permute-start.1
  305.7 9.9 %collective-permute-done.1 = s32[128]{0:T(128)S(1)} collective-permute-done((s32[128]{0:T(128)S(1)}, s32[128]{0:T(128)S(1)}, u32[]{:S(2)}, u32[]{:S(2)}) %collective-permute-start.1) | collective-permute-done | bytes 544 | tf_op jit(solution)/shard_map/while/body/eval_jaxpr/ppermute | solution.py:14
  315.7 1.9 collective-permute-start
  317.6 1.9 collective-permute-start.1
  319.6 10.9 %collective-permute-done.1 = s32[128]{0:T(128)S(1)} collective-permute-done((s32[128]{0:T(128)S(1)}, s32[128]{0:T(128)S(1)}, u32[]{:S(2)}, u32[]{:S(2)}) %collective-permute-start.1) | collective-permute-done | bytes 544 | tf_op jit(solution)/shard_map/while/body/eval_jaxpr/ppermute | solution.py:14
  330.6 1.9 collective-permute-start
  332.5 1.9 collective-permute-start.1
  334.5 9.9 %collective-permute-done.1 = s32[128]{0:T(128)S(1)} collective-permute-done((s32[128]{0:T(128)S(1)}, s32[128]{0:T(128)S(1)}, u32[]{:S(2)}, u32[]{:S(2)}) %collective-permute-start.1) | collective-permute-done | bytes 544 | tf_op jit(solution)/shard_map/while/body/eval_jaxpr/ppermute | solution.py:14
  344.4 1.9 collective-permute-start
  346.4 1.9 collective-permute-start.1
  348.3 9.9 %collective-permute-done.1 = s32[128]{0:T(128)S(1)} collective-permute-done((s32[128]{0:T(128)S(1)}, s32[128]{0:T(128)S(1)}, u32[]{:S(2)}, u32[]{:S(2)}) %collective-permute-start.1) | collective-permute-done | bytes 544 | tf_op jit(solution)/shard_map/while/body/eval_jaxpr/ppermute | solution.py:14
  358.3 1.9 collective-permute-start
  360.2 1.9 collective-permute-start.1
  362.1 9.9 %collective-permute-done.1 = s32[128]{0:T(128)S(1)} collective-permute-done((s32[128]{0:T(128)S(1)}, s32[128]{0:T(128)S(1)}, u32[]{:S(2)}, u32[]{:S(2)}) %collective-permute-start.1) | collective-permute-done | bytes 544 | tf_op jit(solution)/shard_map/while/body/eval_jaxpr/ppermute | solution.py:14
  372.1 1.9 collective-permute-start
  374.0 1.9 collective-permute-start.1
  375.9 9.9 %collective-permute-done.1 = s32[128]{0:T(128)S(1)} collective-permute-done((s32[128]{0:T(128)S(1)}, s32[128]{0:T(128)S(1)}, u32[]{:S(2)}, u32[]{:S(2)}) %collective-permute-start.1) | collective-permute-done | bytes 544 | tf_op jit(solution)/shard_map/while/body/eval_jaxpr/ppermute | solution.py:14
  386.0 1.9 collective-permute-start
  387.9 1.9 collective-permute-start.1
  389.8 11.0 %collective-permute-done.1 = s32[128]{0:T(128)S(1)} collective-permute-done((s32[128]{0:T(128)S(1)}, s32[128]{0:T(128)S(1)}, u32[]{:S(2)}, u32[]{:S(2)}) %collective-permute-start.1) | collective-permute-done | bytes 544 | tf_op jit(solution)/shard_map/while/body/eval_jaxpr/ppermute | solution.py:14
  400.9 1.9 collective-permute-start
  402.8 1.9 collective-permute-start.1
  404.8 9.9 %collective-permute-done.1 = s32[128]{0:T(128)S(1)} collective-permute-done((s32[128]{0:T(128)S(1)}, s32[128]{0:T(128)S(1)}, u32[]{:S(2)}, u32[]{:S(2)}) %collective-permute-start.1) | collective-permute-done | bytes 544 | tf_op jit(solution)/shard_map/while/body/eval_jaxpr/ppermute | solution.py:14
  418.6 9.9 %collective-permute-done.1 = s32[128]{0:T(128)S(1)} collective-permute-done((s32[128]{0:T(128)S(1)}, s32[128]{0:T(128)S(1)}, u32[]{:S(2)}, u32[]{:S(2)}) %collective-permute-start.1) | collective-permute-done | bytes 544 | tf_op jit(solution)/shard_map/while/body/eval_jaxpr/ppermute | solution.py:14
  430.5 1.9 collective-permute-start.1
  432.4 9.9 %collective-permute-done.1 = s32[128]{0:T(128)S(1)} collective-permute-done((s32[128]{0:T(128)S(1)}, s32[128]{0:T(128)S(1)}, u32[]{:S(2)}, u32[]{:S(2)}) %collective-permute-start.1) | collective-permute-done | bytes 544 | tf_op jit(solution)/shard_map/while/body/eval_jaxpr/ppermute | solution.py:14
  446.2 9.9 %collective-permute-done.1 = s32[128]{0:T(128)S(1)} collective-permute-done((s32[128]{0:T(128)S(1)}, s32[128]{0:T(128)S(1)}, u32[]{:S(2)}, u32[]{:S(2)}) %collective-permute-start.1) | collective-permute-done | bytes 544 | tf_op jit(solution)/shard_map/while/body/eval_jaxpr/ppermute | solution.py:14
  456.2 1.9 collective-permute-start
  458.1 1.9 collective-permute-start.1
  460.1 9.9 %collective-permute-done.1 = s32[128]{0:T(128)S(1)} collective-permute-done((s32[128]{0:T(128)S(1)}, s32[128]{0:T(128)S(1)}, u32[]{:S(2)}, u32[]{:S(2)}) %collective-permute-start.1) | collective-permute-done | bytes 544 | tf_op jit(solution)/shard_map/while/body/eval_jaxpr/ppermute | solution.py:14
  473.9 9.9 %collective-permute-done.1 = s32[128]{0:T(128)S(1)} collective-permute-done((s32[128]{0:T(128)S(1)}, s32[128]{0:T(128)S(1)}, u32[]{:S(2)}, u32[]{:S(2)}) %collective-permute-start.1) | collective-permute-done | bytes 544 | tf_op jit(solution)/shard_map/while/body/eval_jaxpr/ppermute | solution.py:14
  483.9 1.9 collective-permute-start
  485.8 1.9 collective-permute-start.1
  487.7 9.9 %collective-permute-done.1 = s32[128]{0:T(128)S(1)} collective-permute-done((s32[128]{0:T(128)S(1)}, s32[128]{0:T(128)S(1)}, u32[]{:S(2)}, u32[]{:S(2)}) %collective-permute-start.1) | collective-permute-done | bytes 544 | tf_op jit(solution)/shard_map/while/body/eval_jaxpr/ppermute | solution.py:14
  501.5 9.9 %collective-permute-done.1 = s32[128]{0:T(128)S(1)} collective-permute-done((s32[128]{0:T(128)S(1)}, s32[128]{0:T(128)S(1)}, u32[]{:S(2)}, u32[]{:S(2)}) %collective-permute-start.1) | collective-permute-done | bytes 544 | tf_op jit(solution)/shard_map/while/body/eval_jaxpr/ppermute | solution.py:14
  515.1 3.6 reshape.168
  520.9 33.3 %reduce-scatter.4.cloned.1.call-done = bf16[640,128]{1,0:T(8,128)(2,1)} async-done(((bf16[2560,128]{1,0:T(8,128)(2,1)}), bf16[640,128]{1,0:T(8,128)(2,1)}) %reduce-scatter.4.cloned.1.call-update) | async-done | bytes 163856
  (157 shorter events, 37.5 us)
Async XLA Ops:
  7.2 53.7 %copy-start.6 = (s32[128]{0:T(128)S(1)}, s32[128]{0:T(128)}, u32[]{:S(2)}) copy-start(s32[128]{0:T(128)} %param.9) | copy-start | bytes 1540
  7.2 21.7 %copy-start.4 = (bf16[2560]{0:T(1024)(128)(2,1)S(1)}, bf16[2560]{0:T(1024)(128)(2,1)}, u32[]{:S(2)}) copy-start(bf16[2560]{0:T(1024)(128)(2,1)} %param.10) | copy-start | bytes 15364
  7.2 140.8 %all-gather.7.cloned.1.call-start = ((), (), s32[]{:S(2)}) async-start(), calls=%async_computation.1 | async-start | bytes 3170304 | tf_op jit(solution)/shard_map/all_gather | solution.py:61
  7.9 272.1 %all-gather.9.cloned.1.call-start = ((), (), s32[]{:S(2)}) async-start(), calls=%async_computation.2 | async-start | bytes 3170304 | tf_op jit(solution)/shard_map/all_gather | solution.py:56
  8.7 506.4 %all-gather.11.cloned.1.call-start = ((), (), s32[]{:S(2)}) async-start(), calls=%async_computation.3 | async-start | bytes 3170304 | tf_op jit(solution)/shard_map/all_gather | solution.py:108
  9.4 544.8 %reduce-scatter.4.cloned.1.call-start = ((), (), s32[]{:S(2)}) async-start(), calls=%async_computation.4 | async-start | bytes 819200
  28.9 122.7 %copy-start.5 = (f32[128]{0:T(128)}, f32[128]{0:T(128)S(1)}, u32[]{:S(2)}) copy-start(f32[128]{0:T(128)S(1)} %add_rsqrt_fusion) | copy-start | bytes 1540
  286.9 227.7 %copy-start.1 = (bf16[128,512]{1,0:T(8,128)(2,1)}, bf16[128,512]{1,0:T(8,128)(2,1)S(1)}, u32[]{:S(2)}) copy-start(bf16[128,512]{1,0:T(8,128)(2,1)S(1)} %copy.19) | copy-start | bytes 393220
  287.0 0.7 copy-start.8
  287.7 223.9 %copy-start.7 = (s32[128]{0:T(128)S(1)}, s32[128]{0:T(128)}, u32[]{:S(2)}) copy-start(s32[128]{0:T(128)} %param.9) | copy-start | bytes 1540
  287.7 224.1 %copy-start.2 = (f32[128,64]{1,0:T(8,128)S(1)}, f32[128,64]{1,0:T(8,128)}, u32[]{:S(2)}) copy-start(f32[128,64]{1,0:T(8,128)} %get-tuple-element.122) | copy-start | bytes 98308
  287.7 224.1 %copy-start.3 = (f32[128,64]{1,0:T(8,128)S(1)}, f32[128,64]{1,0:T(8,128)}, u32[]{:S(2)}) copy-start(f32[128,64]{1,0:T(8,128)} %get-tuple-element.123) | copy-start | bytes 98308
  287.7 14.1 %collective-permute-start = (bf16[128,512]{1,0:T(8,128)(2,1)S(1)}, bf16[128,512]{1,0:T(8,128)(2,1)S(1)}, u32[]{:S(2)}, u32[]{:S(2)}) collective-permute-start(bf16[128,512]{1,0:T(8,128)(2,1)S(1)} %get-tuple-element.171), channel_id=1, source_target_pairs={{0,4},{4,8},{8,12},{12,16},{16,20},{20,24},{24,28},{28,32},{32,36}... | collective-permute-start | bytes 393224 | tf_op jit(solution)/shard_map/while/body/eval_jaxpr/ppermute | solution.py:14
  289.9 11.8 %collective-permute-start.1 = (s32[128]{0:T(128)S(1)}, s32[128]{0:T(128)S(1)}, u32[]{:S(2)}, u32[]{:S(2)}) collective-permute-start(s32[128]{0:T(128)S(1)} %get-tuple-element.172), channel_id=1, source_target_pairs={{0,4},{4,8},{8,12},{12,16},{16,20},{20,24},{24,28},{28,32},{32,36}... | collective-permute-start | bytes 1544 | tf_op jit(solution)/shard_map/while/body/eval_jaxpr/ppermute | solution.py:14
  301.8 13.8 %collective-permute-start = (bf16[128,512]{1,0:T(8,128)(2,1)S(1)}, bf16[128,512]{1,0:T(8,128)(2,1)S(1)}, u32[]{:S(2)}, u32[]{:S(2)}) collective-permute-start(bf16[128,512]{1,0:T(8,128)(2,1)S(1)} %get-tuple-element.171), channel_id=1, source_target_pairs={{0,4},{4,8},{8,12},{12,16},{16,20},{20,24},{24,28},{28,32},{32,36}... | collective-permute-start | bytes 393224 | tf_op jit(solution)/shard_map/while/body/eval_jaxpr/ppermute | solution.py:14
  303.8 11.9 %collective-permute-start.1 = (s32[128]{0:T(128)S(1)}, s32[128]{0:T(128)S(1)}, u32[]{:S(2)}, u32[]{:S(2)}) collective-permute-start(s32[128]{0:T(128)S(1)} %get-tuple-element.172), channel_id=1, source_target_pairs={{0,4},{4,8},{8,12},{12,16},{16,20},{20,24},{24,28},{28,32},{32,36}... | collective-permute-start | bytes 1544 | tf_op jit(solution)/shard_map/while/body/eval_jaxpr/ppermute | solution.py:14
  315.7 14.8 %collective-permute-start = (bf16[128,512]{1,0:T(8,128)(2,1)S(1)}, bf16[128,512]{1,0:T(8,128)(2,1)S(1)}, u32[]{:S(2)}, u32[]{:S(2)}) collective-permute-start(bf16[128,512]{1,0:T(8,128)(2,1)S(1)} %get-tuple-element.171), channel_id=1, source_target_pairs={{0,4},{4,8},{8,12},{12,16},{16,20},{20,24},{24,28},{28,32},{32,36}... | collective-permute-start | bytes 393224 | tf_op jit(solution)/shard_map/while/body/eval_jaxpr/ppermute | solution.py:14
  317.6 12.9 %collective-permute-start.1 = (s32[128]{0:T(128)S(1)}, s32[128]{0:T(128)S(1)}, u32[]{:S(2)}, u32[]{:S(2)}) collective-permute-start(s32[128]{0:T(128)S(1)} %get-tuple-element.172), channel_id=1, source_target_pairs={{0,4},{4,8},{8,12},{12,16},{16,20},{20,24},{24,28},{28,32},{32,36}... | collective-permute-start | bytes 1544 | tf_op jit(solution)/shard_map/while/body/eval_jaxpr/ppermute | solution.py:14
  330.6 13.8 %collective-permute-start = (bf16[128,512]{1,0:T(8,128)(2,1)S(1)}, bf16[128,512]{1,0:T(8,128)(2,1)S(1)}, u32[]{:S(2)}, u32[]{:S(2)}) collective-permute-start(bf16[128,512]{1,0:T(8,128)(2,1)S(1)} %get-tuple-element.171), channel_id=1, source_target_pairs={{0,4},{4,8},{8,12},{12,16},{16,20},{20,24},{24,28},{28,32},{32,36}... | collective-permute-start | bytes 393224 | tf_op jit(solution)/shard_map/while/body/eval_jaxpr/ppermute | solution.py:14
  332.5 11.8 %collective-permute-start.1 = (s32[128]{0:T(128)S(1)}, s32[128]{0:T(128)S(1)}, u32[]{:S(2)}, u32[]{:S(2)}) collective-permute-start(s32[128]{0:T(128)S(1)} %get-tuple-element.172), channel_id=1, source_target_pairs={{0,4},{4,8},{8,12},{12,16},{16,20},{20,24},{24,28},{28,32},{32,36}... | collective-permute-start | bytes 1544 | tf_op jit(solution)/shard_map/while/body/eval_jaxpr/ppermute | solution.py:14
  344.4 13.8 %collective-permute-start = (bf16[128,512]{1,0:T(8,128)(2,1)S(1)}, bf16[128,512]{1,0:T(8,128)(2,1)S(1)}, u32[]{:S(2)}, u32[]{:S(2)}) collective-permute-start(bf16[128,512]{1,0:T(8,128)(2,1)S(1)} %get-tuple-element.171), channel_id=1, source_target_pairs={{0,4},{4,8},{8,12},{12,16},{16,20},{20,24},{24,28},{28,32},{32,36}... | collective-permute-start | bytes 393224 | tf_op jit(solution)/shard_map/while/body/eval_jaxpr/ppermute | solution.py:14
  346.4 11.8 %collective-permute-start.1 = (s32[128]{0:T(128)S(1)}, s32[128]{0:T(128)S(1)}, u32[]{:S(2)}, u32[]{:S(2)}) collective-permute-start(s32[128]{0:T(128)S(1)} %get-tuple-element.172), channel_id=1, source_target_pairs={{0,4},{4,8},{8,12},{12,16},{16,20},{20,24},{24,28},{28,32},{32,36}... | collective-permute-start | bytes 1544 | tf_op jit(solution)/shard_map/while/body/eval_jaxpr/ppermute | solution.py:14
  358.3 13.8 %collective-permute-start = (bf16[128,512]{1,0:T(8,128)(2,1)S(1)}, bf16[128,512]{1,0:T(8,128)(2,1)S(1)}, u32[]{:S(2)}, u32[]{:S(2)}) collective-permute-start(bf16[128,512]{1,0:T(8,128)(2,1)S(1)} %get-tuple-element.171), channel_id=1, source_target_pairs={{0,4},{4,8},{8,12},{12,16},{16,20},{20,24},{24,28},{28,32},{32,36}... | collective-permute-start | bytes 393224 | tf_op jit(solution)/shard_map/while/body/eval_jaxpr/ppermute | solution.py:14
  360.2 11.8 %collective-permute-start.1 = (s32[128]{0:T(128)S(1)}, s32[128]{0:T(128)S(1)}, u32[]{:S(2)}, u32[]{:S(2)}) collective-permute-start(s32[128]{0:T(128)S(1)} %get-tuple-element.172), channel_id=1, source_target_pairs={{0,4},{4,8},{8,12},{12,16},{16,20},{20,24},{24,28},{28,32},{32,36}... | collective-permute-start | bytes 1544 | tf_op jit(solution)/shard_map/while/body/eval_jaxpr/ppermute | solution.py:14
  372.1 13.8 %collective-permute-start = (bf16[128,512]{1,0:T(8,128)(2,1)S(1)}, bf16[128,512]{1,0:T(8,128)(2,1)S(1)}, u32[]{:S(2)}, u32[]{:S(2)}) collective-permute-start(bf16[128,512]{1,0:T(8,128)(2,1)S(1)} %get-tuple-element.171), channel_id=1, source_target_pairs={{0,4},{4,8},{8,12},{12,16},{16,20},{20,24},{24,28},{28,32},{32,36}... | collective-permute-start | bytes 393224 | tf_op jit(solution)/shard_map/while/body/eval_jaxpr/ppermute | solution.py:14
  374.0 11.9 %collective-permute-start.1 = (s32[128]{0:T(128)S(1)}, s32[128]{0:T(128)S(1)}, u32[]{:S(2)}, u32[]{:S(2)}) collective-permute-start(s32[128]{0:T(128)S(1)} %get-tuple-element.172), channel_id=1, source_target_pairs={{0,4},{4,8},{8,12},{12,16},{16,20},{20,24},{24,28},{28,32},{32,36}... | collective-permute-start | bytes 1544 | tf_op jit(solution)/shard_map/while/body/eval_jaxpr/ppermute | solution.py:14
  386.0 14.9 %collective-permute-start = (bf16[128,512]{1,0:T(8,128)(2,1)S(1)}, bf16[128,512]{1,0:T(8,128)(2,1)S(1)}, u32[]{:S(2)}, u32[]{:S(2)}) collective-permute-start(bf16[128,512]{1,0:T(8,128)(2,1)S(1)} %get-tuple-element.171), channel_id=1, source_target_pairs={{0,4},{4,8},{8,12},{12,16},{16,20},{20,24},{24,28},{28,32},{32,36}... | collective-permute-start | bytes 393224 | tf_op jit(solution)/shard_map/while/body/eval_jaxpr/ppermute | solution.py:14
  387.9 12.9 %collective-permute-start.1 = (s32[128]{0:T(128)S(1)}, s32[128]{0:T(128)S(1)}, u32[]{:S(2)}, u32[]{:S(2)}) collective-permute-start(s32[128]{0:T(128)S(1)} %get-tuple-element.172), channel_id=1, source_target_pairs={{0,4},{4,8},{8,12},{12,16},{16,20},{20,24},{24,28},{28,32},{32,36}... | collective-permute-start | bytes 1544 | tf_op jit(solution)/shard_map/while/body/eval_jaxpr/ppermute | solution.py:14
  400.9 13.8 %collective-permute-start = (bf16[128,512]{1,0:T(8,128)(2,1)S(1)}, bf16[128,512]{1,0:T(8,128)(2,1)S(1)}, u32[]{:S(2)}, u32[]{:S(2)}) collective-permute-start(bf16[128,512]{1,0:T(8,128)(2,1)S(1)} %get-tuple-element.171), channel_id=1, source_target_pairs={{0,4},{4,8},{8,12},{12,16},{16,20},{20,24},{24,28},{28,32},{32,36}... | collective-permute-start | bytes 393224 | tf_op jit(solution)/shard_map/while/body/eval_jaxpr/ppermute | solution.py:14
  402.8 11.8 %collective-permute-start.1 = (s32[128]{0:T(128)S(1)}, s32[128]{0:T(128)S(1)}, u32[]{:S(2)}, u32[]{:S(2)}) collective-permute-start(s32[128]{0:T(128)S(1)} %get-tuple-element.172), channel_id=1, source_target_pairs={{0,4},{4,8},{8,12},{12,16},{16,20},{20,24},{24,28},{28,32},{32,36}... | collective-permute-start | bytes 1544 | tf_op jit(solution)/shard_map/while/body/eval_jaxpr/ppermute | solution.py:14
  414.7 13.8 %collective-permute-start = (bf16[128,512]{1,0:T(8,128)(2,1)S(1)}, bf16[128,512]{1,0:T(8,128)(2,1)S(1)}, u32[]{:S(2)}, u32[]{:S(2)}) collective-permute-start(bf16[128,512]{1,0:T(8,128)(2,1)S(1)} %get-tuple-element.171), channel_id=1, source_target_pairs={{0,4},{4,8},{8,12},{12,16},{16,20},{20,24},{24,28},{28,32},{32,36}... | collective-permute-start | bytes 393224 | tf_op jit(solution)/shard_map/while/body/eval_jaxpr/ppermute | solution.py:14
  416.7 11.8 %collective-permute-start.1 = (s32[128]{0:T(128)S(1)}, s32[128]{0:T(128)S(1)}, u32[]{:S(2)}, u32[]{:S(2)}) collective-permute-start(s32[128]{0:T(128)S(1)} %get-tuple-element.172), channel_id=1, source_target_pairs={{0,4},{4,8},{8,12},{12,16},{16,20},{20,24},{24,28},{28,32},{32,36}... | collective-permute-start | bytes 1544 | tf_op jit(solution)/shard_map/while/body/eval_jaxpr/ppermute | solution.py:14
  428.6 13.8 %collective-permute-start = (bf16[128,512]{1,0:T(8,128)(2,1)S(1)}, bf16[128,512]{1,0:T(8,128)(2,1)S(1)}, u32[]{:S(2)}, u32[]{:S(2)}) collective-permute-start(bf16[128,512]{1,0:T(8,128)(2,1)S(1)} %get-tuple-element.171), channel_id=1, source_target_pairs={{0,4},{4,8},{8,12},{12,16},{16,20},{20,24},{24,28},{28,32},{32,36}... | collective-permute-start | bytes 393224 | tf_op jit(solution)/shard_map/while/body/eval_jaxpr/ppermute | solution.py:14
  430.5 11.8 %collective-permute-start.1 = (s32[128]{0:T(128)S(1)}, s32[128]{0:T(128)S(1)}, u32[]{:S(2)}, u32[]{:S(2)}) collective-permute-start(s32[128]{0:T(128)S(1)} %get-tuple-element.172), channel_id=1, source_target_pairs={{0,4},{4,8},{8,12},{12,16},{16,20},{20,24},{24,28},{28,32},{32,36}... | collective-permute-start | bytes 1544 | tf_op jit(solution)/shard_map/while/body/eval_jaxpr/ppermute | solution.py:14
  442.4 13.8 %collective-permute-start = (bf16[128,512]{1,0:T(8,128)(2,1)S(1)}, bf16[128,512]{1,0:T(8,128)(2,1)S(1)}, u32[]{:S(2)}, u32[]{:S(2)}) collective-permute-start(bf16[128,512]{1,0:T(8,128)(2,1)S(1)} %get-tuple-element.171), channel_id=1, source_target_pairs={{0,4},{4,8},{8,12},{12,16},{16,20},{20,24},{24,28},{28,32},{32,36}... | collective-permute-start | bytes 393224 | tf_op jit(solution)/shard_map/while/body/eval_jaxpr/ppermute | solution.py:14
  444.3 11.8 %collective-permute-start.1 = (s32[128]{0:T(128)S(1)}, s32[128]{0:T(128)S(1)}, u32[]{:S(2)}, u32[]{:S(2)}) collective-permute-start(s32[128]{0:T(128)S(1)} %get-tuple-element.172), channel_id=1, source_target_pairs={{0,4},{4,8},{8,12},{12,16},{16,20},{20,24},{24,28},{28,32},{32,36}... | collective-permute-start | bytes 1544 | tf_op jit(solution)/shard_map/while/body/eval_jaxpr/ppermute | solution.py:14
  456.2 13.8 %collective-permute-start = (bf16[128,512]{1,0:T(8,128)(2,1)S(1)}, bf16[128,512]{1,0:T(8,128)(2,1)S(1)}, u32[]{:S(2)}, u32[]{:S(2)}) collective-permute-start(bf16[128,512]{1,0:T(8,128)(2,1)S(1)} %get-tuple-element.171), channel_id=1, source_target_pairs={{0,4},{4,8},{8,12},{12,16},{16,20},{20,24},{24,28},{28,32},{32,36}... | collective-permute-start | bytes 393224 | tf_op jit(solution)/shard_map/while/body/eval_jaxpr/ppermute | solution.py:14
  458.1 11.8 %collective-permute-start.1 = (s32[128]{0:T(128)S(1)}, s32[128]{0:T(128)S(1)}, u32[]{:S(2)}, u32[]{:S(2)}) collective-permute-start(s32[128]{0:T(128)S(1)} %get-tuple-element.172), channel_id=1, source_target_pairs={{0,4},{4,8},{8,12},{12,16},{16,20},{20,24},{24,28},{28,32},{32,36}... | collective-permute-start | bytes 1544 | tf_op jit(solution)/shard_map/while/body/eval_jaxpr/ppermute | solution.py:14
  470.0 13.8 %collective-permute-start = (bf16[128,512]{1,0:T(8,128)(2,1)S(1)}, bf16[128,512]{1,0:T(8,128)(2,1)S(1)}, u32[]{:S(2)}, u32[]{:S(2)}) collective-permute-start(bf16[128,512]{1,0:T(8,128)(2,1)S(1)} %get-tuple-element.171), channel_id=1, source_target_pairs={{0,4},{4,8},{8,12},{12,16},{16,20},{20,24},{24,28},{28,32},{32,36}... | collective-permute-start | bytes 393224 | tf_op jit(solution)/shard_map/while/body/eval_jaxpr/ppermute | solution.py:14
  472.0 11.8 %collective-permute-start.1 = (s32[128]{0:T(128)S(1)}, s32[128]{0:T(128)S(1)}, u32[]{:S(2)}, u32[]{:S(2)}) collective-permute-start(s32[128]{0:T(128)S(1)} %get-tuple-element.172), channel_id=1, source_target_pairs={{0,4},{4,8},{8,12},{12,16},{16,20},{20,24},{24,28},{28,32},{32,36}... | collective-permute-start | bytes 1544 | tf_op jit(solution)/shard_map/while/body/eval_jaxpr/ppermute | solution.py:14
  483.9 13.8 %collective-permute-start = (bf16[128,512]{1,0:T(8,128)(2,1)S(1)}, bf16[128,512]{1,0:T(8,128)(2,1)S(1)}, u32[]{:S(2)}, u32[]{:S(2)}) collective-permute-start(bf16[128,512]{1,0:T(8,128)(2,1)S(1)} %get-tuple-element.171), channel_id=1, source_target_pairs={{0,4},{4,8},{8,12},{12,16},{16,20},{20,24},{24,28},{28,32},{32,36}... | collective-permute-start | bytes 393224 | tf_op jit(solution)/shard_map/while/body/eval_jaxpr/ppermute | solution.py:14
  485.8 11.8 %collective-permute-start.1 = (s32[128]{0:T(128)S(1)}, s32[128]{0:T(128)S(1)}, u32[]{:S(2)}, u32[]{:S(2)}) collective-permute-start(s32[128]{0:T(128)S(1)} %get-tuple-element.172), channel_id=1, source_target_pairs={{0,4},{4,8},{8,12},{12,16},{16,20},{20,24},{24,28},{28,32},{32,36}... | collective-permute-start | bytes 1544 | tf_op jit(solution)/shard_map/while/body/eval_jaxpr/ppermute | solution.py:14
  497.7 13.8 %collective-permute-start = (bf16[128,512]{1,0:T(8,128)(2,1)S(1)}, bf16[128,512]{1,0:T(8,128)(2,1)S(1)}, u32[]{:S(2)}, u32[]{:S(2)}) collective-permute-start(bf16[128,512]{1,0:T(8,128)(2,1)S(1)} %get-tuple-element.171), channel_id=1, source_target_pairs={{0,4},{4,8},{8,12},{12,16},{16,20},{20,24},{24,28},{28,32},{32,36}... | collective-permute-start | bytes 393224 | tf_op jit(solution)/shard_map/while/body/eval_jaxpr/ppermute | solution.py:14
  499.6 11.8 %collective-permute-start.1 = (s32[128]{0:T(128)S(1)}, s32[128]{0:T(128)S(1)}, u32[]{:S(2)}, u32[]{:S(2)}) collective-permute-start(s32[128]{0:T(128)S(1)} %get-tuple-element.172), channel_id=1, source_target_pairs={{0,4},{4,8},{8,12},{12,16},{16,20},{20,24},{24,28},{28,32},{32,36}... | collective-permute-start | bytes 1544 | tf_op jit(solution)/shard_map/while/body/eval_jaxpr/ppermute | solution.py:14
  511.5 0.6 copy-start.9
  519.7 35.5 %copy-start = (bf16[128,640]{1,0:T(8,128)(2,1)S(1)}, bf16[128,640]{1,0:T(8,128)(2,1)}, u32[]{:S(2)}) copy-start(bf16[128,640]{1,0:T(8,128)(2,1)} %param.8) | copy-start | bytes 491524
Sparse Core Ops, SparseCore 0:
  12.7 135.2 all-gather.6
  152.7 127.3 all-gather.8
  284.8 126.9 all-gather.10
  521.0 33.1 reduce-scatter.3
where the time goes:
time: 564 us; the launch traced here: 562 us
  waiting for transfers between devices  406 us (72%)
  starting transfers between devices  62.4 us (11%)
  blocking collectives  50.3 us (9%)
  local copies, waits for them, and re-layouts  16.6 us (3%)
  between operations  14.1 us (2%)
  other arithmetic  6.51 us (1%)
  matrix products  5.67 us (1%)
    ppermute x32, waiting for transfers between devices, from_behind(): return lax.ppermute(x, axis, pairs)  160 us
    all_gather x1, waiting for transfers between devices, per_device(): lax.all_gather(w_query, 'seq', axis=0, tiled=True)  125 us
    all_gather x1, waiting for transfers between devices, per_device(): lax.all_gather(w_keyval, 'seq', axis=0, tiled=True)  85.6 us
    ppermute x32, starting transfers between devices, from_behind(): return lax.ppermute(x, axis, pairs)  62.3 us
    unnamed x5, waiting for transfers between devices  35.4 us
    psum x1, blocking collectives, per_device(): starts = lax.psum(below, 'seq')  31.9 us
    all_gather x1, blocking collectives, per_device(): gathered = lax.all_gather(tokens, 'tp', axis=1, tiled=True)  18.5 us
    unnamed x27, local copies, waits for them, and re-layouts  13.8 us
  transfers between devices with their start and end apart: 36, of which 19 were waited for; matrix products, arithmetic and copies ran while one was open for 4% of the time, Pallas kernels for 0%

commit v1 on v0

--- a/solution.py
+++ b/solution.py
@@ -1,3 +1,4 @@
+import functools
 import jax
 import jax.numpy as jnp
 from jax import lax
@@ -6,6 +7,21 @@
 HD = 256
 WINDOW = 2048
 SEG_MEAN = 512
+
+
+def words_post(x0, chip_axis):
+    return jnp.concatenate(
+        lax.all_to_all(
+            jnp.stack(lax.axis_size(chip_axis) * [x0], 0),
+            axis_name=chip_axis,
+            split_axis=0,
+            concat_axis=0,
+        ),
+        0,
+    )
+
+
+resolve_teams = functools.partial(words_post, chip_axis="seq")
 
 
 def from_behind(x, axis, by):
@@ -51,11 +67,7 @@
     own_start = jnp.sum(jnp.where(seg_ids[:, None] == labels[None, :], starts[None, :], 0), axis=1)
     token_index = my_index * tok_rows + jnp.arange(tok_rows, dtype=jnp.int32)
     positions = (token_index - own_start).astype(jnp.float32)
-    query_raw = jnp.dot(
-        normed,
-        lax.all_gather(w_query, "seq", axis=0, tiled=True),
-        preferred_element_type=jnp.float32,
-    )
+    query_raw = jnp.dot(normed, resolve_teams(w_query), preferred_element_type=jnp.float32)
     keyval_raw = jnp.dot(
         normed,
         lax.all_gather(w_keyval, "seq", axis=0, tiled=True),

time: 564 us -> 612 us (1.085)
  waiting for transfers between devices: 406 us -> 345 us
  blocking collectives: 50.3 us -> 109 us
  local copies, waits for them, and re-layouts: 16.6 us -> 47.7 us
  starting transfers between devices: 62.4 us -> 82.2 us
    all_gather x1 -> x0, waiting for transfers between devices: 125 us -> none  [per_device(): lax.all_gather(w_query, 'seq', axis=0, tiled=True)]
    all_gather x1, waiting for transfers between devices: 0.02 us -> 121 us  [per_device(): lax.all_gather(w_out, 'seq', axis=1, tiled=True)]
    psum x1, blocking collectives: 31.9 us -> 93 us  [per_device(): starts = lax.psum(below, 'seq')]
    all_gather x1, waiting for transfers between devices: 85.6 us -> 38.9 us  [per_device(): lax.all_gather(w_keyval, 'seq', axis=0, tiled=True)]
    all_to_all x0 -> x1, starting transfers between devices: none -> 20.1 us  [words_post(): lax.all_to_all(jnp.stack(lax.axis_size(chip_axis) * [x0], 0), axis_name=c...]
    while x32, local copies, waits for them, and re-layouts: 0.19 us -> 10.6 us
    dynamic_update_slice x16, local copies, waits for them, and re-layouts: 0.25 us -> 10.6 us  [advance(): store = lax.dynamic_update_slice_in_dim(store, current[None], slot, 0)]
    unnamed x5 -> x4, waiting for transfers between devices: 35.4 us -> 26.3 us
  transfers between devices with their start and end apart: 36 -> 36, of which waited for: 19 -> 19; matrix products, arithmetic and copies ran while one was open for 4% -> 7% of each run, Pallas kernels for 0% -> 0%
where the time goes in v1:
time: 612 us; the launch traced here: 610 us
  waiting for transfers between devices  345 us (56%)
  blocking collectives  109 us (18%)
  starting transfers between devices  82.2 us (13%)
  local copies, waits for them, and re-layouts  47.7 us (8%)
  between operations  14 us (2%)
  matrix products  7.4 us (1%)
    ppermute x32, waiting for transfers between devices, from_behind(): return lax.ppermute(x, axis, pairs)  159 us
    all_gather x1, waiting for transfers between devices, per_device(): lax.all_gather(w_out, 'seq', axis=1, tiled=True)  121 us
    psum x1, blocking collectives, per_device(): starts = lax.psum(below, 'seq')  93 us
    ppermute x32, starting transfers between devices, from_behind(): return lax.ppermute(x, axis, pairs)  61.9 us
    all_gather x1, waiting for transfers between devices, per_device(): lax.all_gather(w_keyval, 'seq', axis=0, tiled=True)  38.9 us
    unnamed x4, waiting for transfers between devices  26.3 us
    all_to_all x1, starting transfers between devices, words_post(): lax.all_to_all(jnp.stack(lax.axis_size(chip_axis) * [x0], 0), axis_name=c...  20.1 us
    unnamed x35, local copies, waits for them, and re-layouts  15.8 us
  transfers between devices with their start and end apart: 36, of which 19 were waited for; matrix products, arithmetic and copies ran while one was open for 7% of the time, Pallas kernels for 0%

profile of v1, /device:TPU:2, one launch (start us, length us, event | category | flops | bytes accessed | tf_op | source)
XLA Modules:
  0.0 610.5 jit_solution(13516661169871425369)
XLA Ops:
  8.6 2.6 stack.2
  11.2 20.1 %all-to-all-start = ((bf16[128,20,512]{2,1,0:T(8,128)(2,1)}), bf16[128,20,512]{2,1,0:T(8,128)(2,1)S(1)}, u32[]{:S(2)}, u32[]{:S(2)}) async-start(bf16[128,20,512]{2,1,0:T(8,128)(2,1)} %stack.2), calls=%async_computation | async-start | bytes 6291456 | tf_op jit(solution)/shard_map/all_to_all | solution.py:14
  31.6 93.0 %psum.7 = s32[32]{0:T(128)S(1)} all-reduce(s32[32]{0:T(128)S(1)} %convert_reduce_fusion), channel_id=1, replica_groups=mesh['seq'=128,'tp'=4] {'seq'}, use_global_device_ids=true, to_apply=%region_2.0 | all-reduce | flops 32 | bytes 256 | tf_op jit(solution)/shard_map/psum | solution.py:66
  124.6 15.7 %all_gather.9 = bf16[128,2560]{1,0:T(8,128)(2,1)S(1)} all-gather(bf16[128,640]{1,0:T(8,128)(2,1)S(1)} %copy-done.4), channel_id=1, replica_groups=mesh['seq'=128,'tp'=4] {'tp'}, dimensions={1}, use_global_device_ids=true | all-gather | bytes 819200 | tf_op jit(solution)/shard_map/all_gather | solution.py:61
  142.8 38.9 %all-gather.5.cloned.1.call-done = bf16[128,20,512]{2,1,0:T(8,128)(2,1)} async-done(((bf16[1,20,512]{2,1,0:T(8,128)(2,1)}), bf16[128,20,512]{2,1,0:T(8,128)(2,1)}) %all-gather.5.cloned.1.call-update) | async-done | bytes 2621456 | tf_op jit(solution)/shard_map/all_gather | solution.py:73
  181.7 5.2 reshape.168
  186.9 3.1 fusion.17
  192.7 121.1 %all-gather.7.cloned.1.call-done = bf16[128,20,512]{2,1,0:T(8,128)(2,1)} async-done(((bf16[1,20,512]{2,1,0:T(8,128)(2,1)}), bf16[128,20,512]{2,1,0:T(8,128)(2,1)}) %all-gather.7.cloned.1.call-update) | async-done | bytes 2621456 | tf_op jit(solution)/shard_map/all_gather | solution.py:120
  313.8 5.2 reshape.170
  320.6 242.8 %while.19 = (s32[]{:T(128)}, bf16[128,512]{1,0:T(8,128)(2,1)}, s32[128]{0:T(128)S(1)}, bf16[16,128,512]{2,1,0:T(8,128)(2,1)}, s32[16,128]{1,0:T(8,128)S(1)}, /*index=5*/s32[]{:T(128)}, s32[]{:T(128)}, s32[]{:T(128)}, s32[]{:T(128)}) while((s32[]{:T(128)}, bf16[128,512]{1,0:T(8,128)(2,1)}, s32[128]{0:T(128)S(1)}, ...), condition=%wide.region_5.6_spmd, body=%wide.region_4.5_spmd.sunk | while | flops 6 | bytes 1052899 | solution.py:92
  320.6 2.1 collective-permute-start
  322.7 2.4 collective-permute-start.1
  325.1 9.4 %collective-permute-done.1 = s32[128]{0:T(128)S(1)} collective-permute-done((s32[128]{0:T(128)S(1)}, s32[128]{0:T(128)S(1)}, u32[]{:S(2)}, u32[]{:S(2)}) %collective-permute-start.1) | collective-permute-done | bytes 544 | tf_op jit(solution)/shard_map/while/body/eval_jaxpr/ppermute | solution.py:30
  335.8 1.9 collective-permute-start
  337.8 1.9 collective-permute-start.1
  339.7 9.9 %collective-permute-done.1 = s32[128]{0:T(128)S(1)} collective-permute-done((s32[128]{0:T(128)S(1)}, s32[128]{0:T(128)S(1)}, u32[]{:S(2)}, u32[]{:S(2)}) %collective-permute-start.1) | collective-permute-done | bytes 544 | tf_op jit(solution)/shard_map/while/body/eval_jaxpr/ppermute | solution.py:30
  350.9 1.9 collective-permute-start
  352.8 1.9 collective-permute-start.1
  354.8 11.1 %collective-permute-done.1 = s32[128]{0:T(128)S(1)} collective-permute-done((s32[128]{0:T(128)S(1)}, s32[128]{0:T(128)S(1)}, u32[]{:S(2)}, u32[]{:S(2)}) %collective-permute-start.1) | collective-permute-done | bytes 544 | tf_op jit(solution)/shard_map/while/body/eval_jaxpr/ppermute | solution.py:30
  369.2 1.9 collective-permute-start.1
  371.1 9.9 %collective-permute-done.1 = s32[128]{0:T(128)S(1)} collective-permute-done((s32[128]{0:T(128)S(1)}, s32[128]{0:T(128)S(1)}, u32[]{:S(2)}, u32[]{:S(2)}) %collective-permute-start.1) | collective-permute-done | bytes 544 | tf_op jit(solution)/shard_map/while/body/eval_jaxpr/ppermute | solution.py:30
  384.3 1.9 collective-permute-start.1
  386.2 9.9 %collective-permute-done.1 = s32[128]{0:T(128)S(1)} collective-permute-done((s32[128]{0:T(128)S(1)}, s32[128]{0:T(128)S(1)}, u32[]{:S(2)}, u32[]{:S(2)}) %collective-permute-start.1) | collective-permute-done | bytes 544 | tf_op jit(solution)/shard_map/while/body/eval_jaxpr/ppermute | solution.py:30
  399.4 1.9 collective-permute-start.1
  401.3 9.9 %collective-permute-done.1 = s32[128]{0:T(128)S(1)} collective-permute-done((s32[128]{0:T(128)S(1)}, s32[128]{0:T(128)S(1)}, u32[]{:S(2)}, u32[]{:S(2)}) %collective-permute-start.1) | collective-permute-done | bytes 544 | tf_op jit(solution)/shard_map/while/body/eval_jaxpr/ppermute | solution.py:30
  414.4 1.9 collective-permute-start.1
  416.4 9.9 %collective-permute-done.1 = s32[128]{0:T(128)S(1)} collective-permute-done((s32[128]{0:T(128)S(1)}, s32[128]{0:T(128)S(1)}, u32[]{:S(2)}, u32[]{:S(2)}) %collective-permute-start.1) | collective-permute-done | bytes 544 | tf_op jit(solution)/shard_map/while/body/eval_jaxpr/ppermute | solution.py:30
  429.5 1.9 collective-permute-start.1
  431.5 9.9 %collective-permute-done.1 = s32[128]{0:T(128)S(1)} collective-permute-done((s32[128]{0:T(128)S(1)}, s32[128]{0:T(128)S(1)}, u32[]{:S(2)}, u32[]{:S(2)}) %collective-permute-start.1) | collective-permute-done | bytes 544 | tf_op jit(solution)/shard_map/while/body/eval_jaxpr/ppermute | solution.py:30
  444.6 1.9 collective-permute-start.1
  446.5 9.9 %collective-permute-done.1 = s32[128]{0:T(128)S(1)} collective-permute-done((s32[128]{0:T(128)S(1)}, s32[128]{0:T(128)S(1)}, u32[]{:S(2)}, u32[]{:S(2)}) %collective-permute-start.1) | collective-permute-done | bytes 544 | tf_op jit(solution)/shard_map/while/body/eval_jaxpr/ppermute | solution.py:30
  459.7 1.9 collective-permute-start.1
  461.6 9.9 %collective-permute-done.1 = s32[128]{0:T(128)S(1)} collective-permute-done((s32[128]{0:T(128)S(1)}, s32[128]{0:T(128)S(1)}, u32[]{:S(2)}, u32[]{:S(2)}) %collective-permute-start.1) | collective-permute-done | bytes 544 | tf_op jit(solution)/shard_map/while/body/eval_jaxpr/ppermute | solution.py:30
  474.8 1.9 collective-permute-start.1
  476.7 9.9 %collective-permute-done.1 = s32[128]{0:T(128)S(1)} collective-permute-done((s32[128]{0:T(128)S(1)}, s32[128]{0:T(128)S(1)}, u32[]{:S(2)}, u32[]{:S(2)}) %collective-permute-start.1) | collective-permute-done | bytes 544 | tf_op jit(solution)/shard_map/while/body/eval_jaxpr/ppermute | solution.py:30
  489.8 1.9 collective-permute-start.1
  491.8 9.9 %collective-permute-done.1 = s32[128]{0:T(128)S(1)} collective-permute-done((s32[128]{0:T(128)S(1)}, s32[128]{0:T(128)S(1)}, u32[]{:S(2)}, u32[]{:S(2)}) %collective-permute-start.1) | collective-permute-done | bytes 544 | tf_op jit(solution)/shard_map/while/body/eval_jaxpr/ppermute | solution.py:30
  504.9 1.9 collective-permute-start.1
  506.8 9.9 %collective-permute-done.1 = s32[128]{0:T(128)S(1)} collective-permute-done((s32[128]{0:T(128)S(1)}, s32[128]{0:T(128)S(1)}, u32[]{:S(2)}, u32[]{:S(2)}) %collective-permute-start.1) | collective-permute-done | bytes 544 | tf_op jit(solution)/shard_map/while/body/eval_jaxpr/ppermute | solution.py:30
  520.0 1.9 collective-permute-start.1
  521.9 9.9 %collective-permute-done.1 = s32[128]{0:T(128)S(1)} collective-permute-done((s32[128]{0:T(128)S(1)}, s32[128]{0:T(128)S(1)}, u32[]{:S(2)}, u32[]{:S(2)}) %collective-permute-start.1) | collective-permute-done | bytes 544 | tf_op jit(solution)/shard_map/while/body/eval_jaxpr/ppermute | solution.py:30
  535.1 1.9 collective-permute-start.1
  537.0 9.9 %collective-permute-done.1 = s32[128]{0:T(128)S(1)} collective-permute-done((s32[128]{0:T(128)S(1)}, s32[128]{0:T(128)S(1)}, u32[]{:S(2)}, u32[]{:S(2)}) %collective-permute-start.1) | collective-permute-done | bytes 544 | tf_op jit(solution)/shard_map/while/body/eval_jaxpr/ppermute | solution.py:30
  550.2 1.9 collective-permute-start.1
  552.1 9.9 %collective-permute-done.1 = s32[128]{0:T(128)S(1)} collective-permute-done((s32[128]{0:T(128)S(1)}, s32[128]{0:T(128)S(1)}, u32[]{:S(2)}, u32[]{:S(2)}) %collective-permute-start.1) | collective-permute-done | bytes 544 | tf_op jit(solution)/shard_map/while/body/eval_jaxpr/ppermute | solution.py:30
  564.0 2.2 reshape.165
  566.2 3.0 copy.15
  577.3 24.9 %reduce-scatter.4.cloned.1.call-done = bf16[640,128]{1,0:T(8,128)(2,1)} async-done(((bf16[2560,128]{1,0:T(8,128)(2,1)}), bf16[640,128]{1,0:T(8,128)(2,1)}) %reduce-scatter.4.cloned.1.call-update) | async-done | bytes 163856
  (165 shorter events, 65.1 us)
Async XLA Ops:
  7.2 174.6 %all-gather.5.cloned.1.call-start = ((), (), s32[]{:S(2)}) async-start(), calls=%async_computation.2 | async-start | bytes 3170304 | tf_op jit(solution)/shard_map/all_gather | solution.py:73
  7.9 305.9 %all-gather.7.cloned.1.call-start = ((), (), s32[]{:S(2)}) async-start(), calls=%async_computation.3 | async-start | bytes 3170304 | tf_op jit(solution)/shard_map/all_gather | solution.py:120
  11.2 20.2 %copy-start.11 = (s32[128]{0:T(128)S(1)}, s32[128]{0:T(128)}, u32[]{:S(2)}) copy-start(s32[128]{0:T(128)} %param.9) | copy-start | bytes 1540
  11.2 113.4 %copy-start.4 = (bf16[128,640]{1,0:T(8,128)(2,1)S(1)}, bf16[128,640]{1,0:T(8,128)(2,1)}, u32[]{:S(2)}) copy-start(bf16[128,640]{1,0:T(8,128)(2,1)} %param.8) | copy-start | bytes 491524
  11.2 552.8 %all-to-all-start = ((bf16[128,20,512]{2,1,0:T(8,128)(2,1)}), bf16[128,20,512]{2,1,0:T(8,128)(2,1)S(1)}, u32[]{:S(2)}, u32[]{:S(2)}) async-start(bf16[128,20,512]{2,1,0:T(8,128)(2,1)} %stack.2), calls=%async_computation | async-start | bytes 6291456 | tf_op jit(solution)/shard_map/all_to_all | solution.py:14
  31.4 110.5 %copy-start.8 = (bf16[2560]{0:T(1024)(128)(2,1)S(1)}, bf16[2560]{0:T(1024)(128)(2,1)}, u32[]{:S(2)}) copy-start(bf16[2560]{0:T(1024)(128)(2,1)} %param.10) | copy-start | bytes 15364
  31.4 570.8 %reduce-scatter.4.cloned.1.call-start = ((), (), s32[]{:S(2)}) async-start(), calls=%async_computation.4 | async-start | bytes 819200
  141.3 45.6 %copy-start.9 = (f32[128]{0:T(128)}, f32[128]{0:T(128)S(1)}, u32[]{:S(2)}) copy-start(f32[128]{0:T(128)S(1)} %add_rsqrt_fusion) | copy-start | bytes 1540
  192.0 127.0 %copy-start.5 = (bf16[128,512]{1,0:T(8,128)(2,1)}, bf16[128,512]{1,0:T(8,128)(2,1)S(1)}, u32[]{:S(2)}) copy-start(bf16[128,512]{1,0:T(8,128)(2,1)S(1)} %copy.14) | copy-start | bytes 393220
  320.6 14.0 %collective-permute-start = (bf16[128,512]{1,0:T(8,128)(2,1)}, bf16[128,512]{1,0:T(8,128)(2,1)S(1)}, u32[]{:S(2)}, u32[]{:S(2)}) collective-permute-start(bf16[128,512]{1,0:T(8,128)(2,1)} %get-tuple-element.169), channel_id=1, source_target_pairs={{0,4},{4,8},{8,12},{12,16},{16,20},{20,24},{24,28},{28,32},{32,36}... | collective-permute-start | bytes 393224 | tf_op jit(solution)/shard_map/while/body/eval_jaxpr/ppermute | solution.py:30
  322.7 11.8 %collective-permute-start.1 = (s32[128]{0:T(128)S(1)}, s32[128]{0:T(128)S(1)}, u32[]{:S(2)}, u32[]{:S(2)}) collective-permute-start(s32[128]{0:T(128)S(1)} %get-tuple-element.170), channel_id=1, source_target_pairs={{0,4},{4,8},{8,12},{12,16},{16,20},{20,24},{24,28},{28,32},{32,36}... | collective-permute-start | bytes 1544 | tf_op jit(solution)/shard_map/while/body/eval_jaxpr/ppermute | solution.py:30
  335.8 13.8 %collective-permute-start = (bf16[128,512]{1,0:T(8,128)(2,1)}, bf16[128,512]{1,0:T(8,128)(2,1)S(1)}, u32[]{:S(2)}, u32[]{:S(2)}) collective-permute-start(bf16[128,512]{1,0:T(8,128)(2,1)} %get-tuple-element.169), channel_id=1, source_target_pairs={{0,4},{4,8},{8,12},{12,16},{16,20},{20,24},{24,28},{28,32},{32,36}... | collective-permute-start | bytes 393224 | tf_op jit(solution)/shard_map/while/body/eval_jaxpr/ppermute | solution.py:30
  337.8 11.8 %collective-permute-start.1 = (s32[128]{0:T(128)S(1)}, s32[128]{0:T(128)S(1)}, u32[]{:S(2)}, u32[]{:S(2)}) collective-permute-start(s32[128]{0:T(128)S(1)} %get-tuple-element.170), channel_id=1, source_target_pairs={{0,4},{4,8},{8,12},{12,16},{16,20},{20,24},{24,28},{28,32},{32,36}... | collective-permute-start | bytes 1544 | tf_op jit(solution)/shard_map/while/body/eval_jaxpr/ppermute | solution.py:30
  350.9 15.0 %collective-permute-start = (bf16[128,512]{1,0:T(8,128)(2,1)}, bf16[128,512]{1,0:T(8,128)(2,1)S(1)}, u32[]{:S(2)}, u32[]{:S(2)}) collective-permute-start(bf16[128,512]{1,0:T(8,128)(2,1)} %get-tuple-element.169), channel_id=1, source_target_pairs={{0,4},{4,8},{8,12},{12,16},{16,20},{20,24},{24,28},{28,32},{32,36}... | collective-permute-start | bytes 393224 | tf_op jit(solution)/shard_map/while/body/eval_jaxpr/ppermute | solution.py:30
  352.8 13.1 %collective-permute-start.1 = (s32[128]{0:T(128)S(1)}, s32[128]{0:T(128)S(1)}, u32[]{:S(2)}, u32[]{:S(2)}) collective-permute-start(s32[128]{0:T(128)S(1)} %get-tuple-element.170), channel_id=1, source_target_pairs={{0,4},{4,8},{8,12},{12,16},{16,20},{20,24},{24,28},{28,32},{32,36}... | collective-permute-start | bytes 1544 | tf_op jit(solution)/shard_map/while/body/eval_jaxpr/ppermute | solution.py:30
  367.3 13.8 %collective-permute-start = (bf16[128,512]{1,0:T(8,128)(2,1)}, bf16[128,512]{1,0:T(8,128)(2,1)S(1)}, u32[]{:S(2)}, u32[]{:S(2)}) collective-permute-start(bf16[128,512]{1,0:T(8,128)(2,1)} %get-tuple-element.169), channel_id=1, source_target_pairs={{0,4},{4,8},{8,12},{12,16},{16,20},{20,24},{24,28},{28,32},{32,36}... | collective-permute-start | bytes 393224 | tf_op jit(solution)/shard_map/while/body/eval_jaxpr/ppermute | solution.py:30
  369.2 11.8 %collective-permute-start.1 = (s32[128]{0:T(128)S(1)}, s32[128]{0:T(128)S(1)}, u32[]{:S(2)}, u32[]{:S(2)}) collective-permute-start(s32[128]{0:T(128)S(1)} %get-tuple-element.170), channel_id=1, source_target_pairs={{0,4},{4,8},{8,12},{12,16},{16,20},{20,24},{24,28},{28,32},{32,36}... | collective-permute-start | bytes 1544 | tf_op jit(solution)/shard_map/while/body/eval_jaxpr/ppermute | solution.py:30
  382.4 13.8 %collective-permute-start = (bf16[128,512]{1,0:T(8,128)(2,1)}, bf16[128,512]{1,0:T(8,128)(2,1)S(1)}, u32[]{:S(2)}, u32[]{:S(2)}) collective-permute-start(bf16[128,512]{1,0:T(8,128)(2,1)} %get-tuple-element.169), channel_id=1, source_target_pairs={{0,4},{4,8},{8,12},{12,16},{16,20},{20,24},{24,28},{28,32},{32,36}... | collective-permute-start | bytes 393224 | tf_op jit(solution)/shard_map/while/body/eval_jaxpr/ppermute | solution.py:30
  384.3 11.8 %collective-permute-start.1 = (s32[128]{0:T(128)S(1)}, s32[128]{0:T(128)S(1)}, u32[]{:S(2)}, u32[]{:S(2)}) collective-permute-start(s32[128]{0:T(128)S(1)} %get-tuple-element.170), channel_id=1, source_target_pairs={{0,4},{4,8},{8,12},{12,16},{16,20},{20,24},{24,28},{28,32},{32,36}... | collective-permute-start | bytes 1544 | tf_op jit(solution)/shard_map/while/body/eval_jaxpr/ppermute | solution.py:30
  397.4 13.8 %collective-permute-start = (bf16[128,512]{1,0:T(8,128)(2,1)}, bf16[128,512]{1,0:T(8,128)(2,1)S(1)}, u32[]{:S(2)}, u32[]{:S(2)}) collective-permute-start(bf16[128,512]{1,0:T(8,128)(2,1)} %get-tuple-element.169), channel_id=1, source_target_pairs={{0,4},{4,8},{8,12},{12,16},{16,20},{20,24},{24,28},{28,32},{32,36}... | collective-permute-start | bytes 393224 | tf_op jit(solution)/shard_map/while/body/eval_jaxpr/ppermute | solution.py:30
  399.4 11.8 %collective-permute-start.1 = (s32[128]{0:T(128)S(1)}, s32[128]{0:T(128)S(1)}, u32[]{:S(2)}, u32[]{:S(2)}) collective-permute-start(s32[128]{0:T(128)S(1)} %get-tuple-element.170), channel_id=1, source_target_pairs={{0,4},{4,8},{8,12},{12,16},{16,20},{20,24},{24,28},{28,32},{32,36}... | collective-permute-start | bytes 1544 | tf_op jit(solution)/shard_map/while/body/eval_jaxpr/ppermute | solution.py:30
  412.5 13.8 %collective-permute-start = (bf16[128,512]{1,0:T(8,128)(2,1)}, bf16[128,512]{1,0:T(8,128)(2,1)S(1)}, u32[]{:S(2)}, u32[]{:S(2)}) collective-permute-start(bf16[128,512]{1,0:T(8,128)(2,1)} %get-tuple-element.169), channel_id=1, source_target_pairs={{0,4},{4,8},{8,12},{12,16},{16,20},{20,24},{24,28},{28,32},{32,36}... | collective-permute-start | bytes 393224 | tf_op jit(solution)/shard_map/while/body/eval_jaxpr/ppermute | solution.py:30
  414.4 11.8 %collective-permute-start.1 = (s32[128]{0:T(128)S(1)}, s32[128]{0:T(128)S(1)}, u32[]{:S(2)}, u32[]{:S(2)}) collective-permute-start(s32[128]{0:T(128)S(1)} %get-tuple-element.170), channel_id=1, source_target_pairs={{0,4},{4,8},{8,12},{12,16},{16,20},{20,24},{24,28},{28,32},{32,36}... | collective-permute-start | bytes 1544 | tf_op jit(solution)/shard_map/while/body/eval_jaxpr/ppermute | solution.py:30
  427.6 13.8 %collective-permute-start = (bf16[128,512]{1,0:T(8,128)(2,1)}, bf16[128,512]{1,0:T(8,128)(2,1)S(1)}, u32[]{:S(2)}, u32[]{:S(2)}) collective-permute-start(bf16[128,512]{1,0:T(8,128)(2,1)} %get-tuple-element.169), channel_id=1, source_target_pairs={{0,4},{4,8},{8,12},{12,16},{16,20},{20,24},{24,28},{28,32},{32,36}... | collective-permute-start | bytes 393224 | tf_op jit(solution)/shard_map/while/body/eval_jaxpr/ppermute | solution.py:30
  429.5 11.8 %collective-permute-start.1 = (s32[128]{0:T(128)S(1)}, s32[128]{0:T(128)S(1)}, u32[]{:S(2)}, u32[]{:S(2)}) collective-permute-start(s32[128]{0:T(128)S(1)} %get-tuple-element.170), channel_id=1, source_target_pairs={{0,4},{4,8},{8,12},{12,16},{16,20},{20,24},{24,28},{28,32},{32,36}... | collective-permute-start | bytes 1544 | tf_op jit(solution)/shard_map/while/body/eval_jaxpr/ppermute | solution.py:30
  442.7 13.8 %collective-permute-start = (bf16[128,512]{1,0:T(8,128)(2,1)}, bf16[128,512]{1,0:T(8,128)(2,1)S(1)}, u32[]{:S(2)}, u32[]{:S(2)}) collective-permute-start(bf16[128,512]{1,0:T(8,128)(2,1)} %get-tuple-element.169), channel_id=1, source_target_pairs={{0,4},{4,8},{8,12},{12,16},{16,20},{20,24},{24,28},{28,32},{32,36}... | collective-permute-start | bytes 393224 | tf_op jit(solution)/shard_map/while/body/eval_jaxpr/ppermute | solution.py:30
  444.6 11.8 %collective-permute-start.1 = (s32[128]{0:T(128)S(1)}, s32[128]{0:T(128)S(1)}, u32[]{:S(2)}, u32[]{:S(2)}) collective-permute-start(s32[128]{0:T(128)S(1)} %get-tuple-element.170), channel_id=1, source_target_pairs={{0,4},{4,8},{8,12},{12,16},{16,20},{20,24},{24,28},{28,32},{32,36}... | collective-permute-start | bytes 1544 | tf_op jit(solution)/shard_map/while/body/eval_jaxpr/ppermute | solution.py:30
  457.8 13.8 %collective-permute-start = (bf16[128,512]{1,0:T(8,128)(2,1)}, bf16[128,512]{1,0:T(8,128)(2,1)S(1)}, u32[]{:S(2)}, u32[]{:S(2)}) collective-permute-start(bf16[128,512]{1,0:T(8,128)(2,1)} %get-tuple-element.169), channel_id=1, source_target_pairs={{0,4},{4,8},{8,12},{12,16},{16,20},{20,24},{24,28},{28,32},{32,36}... | collective-permute-start | bytes 393224 | tf_op jit(solution)/shard_map/while/body/eval_jaxpr/ppermute | solution.py:30
  459.7 11.8 %collective-permute-start.1 = (s32[128]{0:T(128)S(1)}, s32[128]{0:T(128)S(1)}, u32[]{:S(2)}, u32[]{:S(2)}) collective-permute-start(s32[128]{0:T(128)S(1)} %get-tuple-element.170), channel_id=1, source_target_pairs={{0,4},{4,8},{8,12},{12,16},{16,20},{20,24},{24,28},{28,32},{32,36}... | collective-permute-start | bytes 1544 | tf_op jit(solution)/shard_map/while/body/eval_jaxpr/ppermute | solution.py:30
  472.8 13.8 %collective-permute-start = (bf16[128,512]{1,0:T(8,128)(2,1)}, bf16[128,512]{1,0:T(8,128)(2,1)S(1)}, u32[]{:S(2)}, u32[]{:S(2)}) collective-permute-start(bf16[128,512]{1,0:T(8,128)(2,1)} %get-tuple-element.169), channel_id=1, source_target_pairs={{0,4},{4,8},{8,12},{12,16},{16,20},{20,24},{24,28},{28,32},{32,36}... | collective-permute-start | bytes 393224 | tf_op jit(solution)/shard_map/while/body/eval_jaxpr/ppermute | solution.py:30
  474.8 11.8 %collective-permute-start.1 = (s32[128]{0:T(128)S(1)}, s32[128]{0:T(128)S(1)}, u32[]{:S(2)}, u32[]{:S(2)}) collective-permute-start(s32[128]{0:T(128)S(1)} %get-tuple-element.170), channel_id=1, source_target_pairs={{0,4},{4,8},{8,12},{12,16},{16,20},{20,24},{24,28},{28,32},{32,36}... | collective-permute-start | bytes 1544 | tf_op jit(solution)/shard_map/while/body/eval_jaxpr/ppermute | solution.py:30
  487.9 13.8 %collective-permute-start = (bf16[128,512]{1,0:T(8,128)(2,1)}, bf16[128,512]{1,0:T(8,128)(2,1)S(1)}, u32[]{:S(2)}, u32[]{:S(2)}) collective-permute-start(bf16[128,512]{1,0:T(8,128)(2,1)} %get-tuple-element.169), channel_id=1, source_target_pairs={{0,4},{4,8},{8,12},{12,16},{16,20},{20,24},{24,28},{28,32},{32,36}... | collective-permute-start | bytes 393224 | tf_op jit(solution)/shard_map/while/body/eval_jaxpr/ppermute | solution.py:30
  489.8 11.8 %collective-permute-start.1 = (s32[128]{0:T(128)S(1)}, s32[128]{0:T(128)S(1)}, u32[]{:S(2)}, u32[]{:S(2)}) collective-permute-start(s32[128]{0:T(128)S(1)} %get-tuple-element.170), channel_id=1, source_target_pairs={{0,4},{4,8},{8,12},{12,16},{16,20},{20,24},{24,28},{28,32},{32,36}... | collective-permute-start | bytes 1544 | tf_op jit(solution)/shard_map/while/body/eval_jaxpr/ppermute | solution.py:30
  503.0 13.8 %collective-permute-start = (bf16[128,512]{1,0:T(8,128)(2,1)}, bf16[128,512]{1,0:T(8,128)(2,1)S(1)}, u32[]{:S(2)}, u32[]{:S(2)}) collective-permute-start(bf16[128,512]{1,0:T(8,128)(2,1)} %get-tuple-element.169), channel_id=1, source_target_pairs={{0,4},{4,8},{8,12},{12,16},{16,20},{20,24},{24,28},{28,32},{32,36}... | collective-permute-start | bytes 393224 | tf_op jit(solution)/shard_map/while/body/eval_jaxpr/ppermute | solution.py:30
  504.9 11.8 %collective-permute-start.1 = (s32[128]{0:T(128)S(1)}, s32[128]{0:T(128)S(1)}, u32[]{:S(2)}, u32[]{:S(2)}) collective-permute-start(s32[128]{0:T(128)S(1)} %get-tuple-element.170), channel_id=1, source_target_pairs={{0,4},{4,8},{8,12},{12,16},{16,20},{20,24},{24,28},{28,32},{32,36}... | collective-permute-start | bytes 1544 | tf_op jit(solution)/shard_map/while/body/eval_jaxpr/ppermute | solution.py:30
  518.1 13.8 %collective-permute-start = (bf16[128,512]{1,0:T(8,128)(2,1)}, bf16[128,512]{1,0:T(8,128)(2,1)S(1)}, u32[]{:S(2)}, u32[]{:S(2)}) collective-permute-start(bf16[128,512]{1,0:T(8,128)(2,1)} %get-tuple-element.169), channel_id=1, source_target_pairs={{0,4},{4,8},{8,12},{12,16},{16,20},{20,24},{24,28},{28,32},{32,36}... | collective-permute-start | bytes 393224 | tf_op jit(solution)/shard_map/while/body/eval_jaxpr/ppermute | solution.py:30
  520.0 11.8 %collective-permute-start.1 = (s32[128]{0:T(128)S(1)}, s32[128]{0:T(128)S(1)}, u32[]{:S(2)}, u32[]{:S(2)}) collective-permute-start(s32[128]{0:T(128)S(1)} %get-tuple-element.170), channel_id=1, source_target_pairs={{0,4},{4,8},{8,12},{12,16},{16,20},{20,24},{24,28},{28,32},{32,36}... | collective-permute-start | bytes 1544 | tf_op jit(solution)/shard_map/while/body/eval_jaxpr/ppermute | solution.py:30
  533.2 13.8 %collective-permute-start = (bf16[128,512]{1,0:T(8,128)(2,1)}, bf16[128,512]{1,0:T(8,128)(2,1)S(1)}, u32[]{:S(2)}, u32[]{:S(2)}) collective-permute-start(bf16[128,512]{1,0:T(8,128)(2,1)} %get-tuple-element.169), channel_id=1, source_target_pairs={{0,4},{4,8},{8,12},{12,16},{16,20},{20,24},{24,28},{28,32},{32,36}... | collective-permute-start | bytes 393224 | tf_op jit(solution)/shard_map/while/body/eval_jaxpr/ppermute | solution.py:30
  535.1 11.8 %collective-permute-start.1 = (s32[128]{0:T(128)S(1)}, s32[128]{0:T(128)S(1)}, u32[]{:S(2)}, u32[]{:S(2)}) collective-permute-start(s32[128]{0:T(128)S(1)} %get-tuple-element.170), channel_id=1, source_target_pairs={{0,4},{4,8},{8,12},{12,16},{16,20},{20,24},{24,28},{28,32},{32,36}... | collective-permute-start | bytes 1544 | tf_op jit(solution)/shard_map/while/body/eval_jaxpr/ppermute | solution.py:30
  548.3 13.8 %collective-permute-start = (bf16[128,512]{1,0:T(8,128)(2,1)}, bf16[128,512]{1,0:T(8,128)(2,1)S(1)}, u32[]{:S(2)}, u32[]{:S(2)}) collective-permute-start(bf16[128,512]{1,0:T(8,128)(2,1)} %get-tuple-element.169), channel_id=1, source_target_pairs={{0,4},{4,8},{8,12},{12,16},{16,20},{20,24},{24,28},{28,32},{32,36}... | collective-permute-start | bytes 393224 | tf_op jit(solution)/shard_map/while/body/eval_jaxpr/ppermute | solution.py:30
  550.2 11.8 %collective-permute-start.1 = (s32[128]{0:T(128)S(1)}, s32[128]{0:T(128)S(1)}, u32[]{:S(2)}, u32[]{:S(2)}) collective-permute-start(s32[128]{0:T(128)S(1)} %get-tuple-element.170), channel_id=1, source_target_pairs={{0,4},{4,8},{8,12},{12,16},{16,20},{20,24},{24,28},{28,32},{32,36}... | collective-permute-start | bytes 1544 | tf_op jit(solution)/shard_map/while/body/eval_jaxpr/ppermute | solution.py:30
  566.2 3.1 copy-start.2
  566.2 3.1 copy-start.10
  569.3 1.6 copy-start.3
  569.3 1.6 copy-start.6
  569.3 1.6 copy-start.12
  569.3 1.6 copy-start.14
  573.4 1.7 copy-start
  (3 other events, 3.5 us)
Sparse Core Ops, SparseCore 0:
  12.7 168.9 all-gather.4
  186.5 127.3 all-gather.6
  577.4 24.7 reduce-scatter.3
